TPU v7x, 256 devices: a whole 4x4x8 slice. The times are simulated.
256 devices in a mesh: dom: 128 (over x, z, y), sub: 2 (over core).
Axes of the slice: x: 4, y: 4, z: 8, core: 2. Of those that a mesh axis runs over, the one named last changes fastest.
Arguments:
- positions: float32 [3, 2097152], P(None, ('dom', 'sub')), may hold values from -6 to 6
- masses: float32 [2097152], P(('dom', 'sub')), may hold values from 0.0005 to 0.005
- old_accel: float32 [3, 2097152], P(None, ('dom', 'sub')), may hold values from -6 to 6
- active: int32 [8192], P('dom'), may hold values from 0 to 1, as said below
- parent_of: int32 [8192], P(('dom', 'sub')), may hold values from 0 to 2047
- parent_centers: float32 [3, 2048], replicated, may hold values from -4 to 4
- local_list: int32 [8192, 8], P('dom'), may hold values from 0 to 63
- near_list: int32 [8192, 8], P('dom'), may hold values from 0 to 1023, as said below
- far_list: int32 [8192, 16], P('dom'), may hold values from 0 to 2047, as said below
- send_ids: int32 [256, 128, 4], P(('dom', 'sub')), may hold values from -1 to 31, as said below
- cell_send_ids: int32 [256, 128, 8], P(('dom', 'sub')), may hold values from -1 to 31, as said below
Outputs:
- accel: float32 [3, 2097152], P(None, ('dom', 'sub'))
- parent_moments: float32 [35, 2048], P(None, 'dom')
Inputs may be any that keep to these rules, and one draw needn't show every extreme that they name: On each device between 1 and 16 of its 32 groups are active, and on some device exactly 16. For device g and chip c, slots 0 to n - 1 of send_ids[g, c] name groups of device g and the others hold -1, with 1 <= n <= 4; n = 4 and n = 1 occur in every draw. For device g and chip c, slots 0 to n - 1 of cell_send_ids[g, c] name groups of device g and the others hold -1, with 1 <= n <= 8; n = 8 and n = 1 occur in every draw. `near_list`: an entry g * 4 + k names slot k of send_ids[g, c], c the chip of the row's group; that slot is never -1. `far_list`: an entry g * 8 + k names slot k of cell_send_ids[g, c], c the chip of the row's group; that slot is never -1.
All inputs are finite; a program needn't handle non-finite values.
Results may differ from a plain program's by a relative error of at most 0.0003.
Values sent between devices are 32-bit elements; how exact they have to be, the bound alone decides.
No kernel may reach another device: no remote copies, remote signals or barrier semaphores. Data moves between devices by JAX's collectives and lax.ppermute only.
A program may use at most 64 MiB of HBM per device.

v0:
```python
import functools

import jax
import jax.numpy as jnp
from jax import lax
from jax.experimental import pallas as pl
from jax.experimental.pallas import tpu as pltpu
from jax.sharding import PartitionSpec as P

BUCKET = 256
NB = 32
RQ = 4
RQC = 8
CELL_LANE = 70
EARLY = 2
USES_BITS = 9
USES = 1 << USES_BITS
SPAN = USES + 16
SOFT_SQ = 0.0025
FAR_SQ = 0.25
F32 = jnp.float32
SMEM = pl.BlockSpec(memory_space=pltpu.SMEM)
VMEM = pl.BlockSpec(memory_space=pltpu.VMEM)


def exponent_rows():
    listing = []
    for degree in range(5):
        for power_x in range(degree, -1, -1):
            for power_y in range(degree - power_x, -1, -1):
                listing.append((power_x, power_y, degree - power_x - power_y))
    return listing


TRIPLES = exponent_rows()
SPOT = {triple: number for number, triple in enumerate(TRIPLES)}
AXES = ((1, 0, 0), (0, 1, 0), (0, 0, 1))


def plus(*triples):
    return tuple(sum(parts) for parts in zip(*triples))


def lanes_of(ref, comp, b):
    return ref[comp : comp + 1, pl.ds(pl.multiple_of(b * BUCKET, BUCKET), BUCKET)]


def monomial_sums(offsets, mass):
    x, y, z = offsets
    known = {(0, 0, 0): mass}
    sums = []
    for triple in TRIPLES:
        if triple not in known:
            axis = next(a for a in range(3) if triple[a] > 0)
            lower = tuple(p - (1 if a == axis else 0) for a, p in enumerate(triple))
            known[triple] = known[lower] * offsets[axis]
        sums.append(jnp.sum(known[triple], axis=1, keepdims=True))
    return sums


def cell_columns(moments, center):
    m = {triple: moments[number] for number, triple in enumerate(TRIPLES)}
    trace1 = [sum(m[plus(e, f, f)] for f in AXES) for e in AXES]
    pairs = [t for t in TRIPLES if sum(t) == 2]
    trace2 = [sum(m[plus(t, f, f)] for f in AXES) for t in pairs]
    full = trace2[0] + trace2[3] + trace2[5]
    scale = (1.0, 1.0, 1.5, 2.5, 4.375)
    columns = [m[t] * scale[sum(t)] for t in TRIPLES]
    columns += center
    columns += [-0.5 * (m[(2, 0, 0)] + m[(0, 2, 0)] + m[(0, 0, 2)])]
    columns += [1.5 * t for t in trace1]
    columns += [3.75 * t for t in trace2]
    columns += [0.375 * full]
    return columns


def spread(columns, lane):
    table = jnp.zeros(lane.shape, F32)
    for number, column in enumerate(columns):
        table = jnp.where(lane == number, column, table)
    return table


def pack_kernel(
    ids_ref,
    cell_ids_ref,
    parent_ref,
    pcent_ref,
    pos_ref,
    mass_ref,
    tiles_ref,
    first_ref,
    second_ref,
    rows,
    about,
    terms,
    cells,
    contrib,
):
    chips = first_ref.shape[0]
    for b in range(NB):
        at = pl.ds(b * BUCKET, BUCKET)
        for comp in range(4):
            row = pos_ref[comp : comp + 1, at] if comp < 3 else mass_ref[0:1, at]
            rows[comp, b : b + 1, :] = row
            tiles_ref[b, 2 * comp : 2 * comp + 1, :] = row[:, :128]
            tiles_ref[b, 2 * comp + 1 : 2 * comp + 2, :] = row[:, 128:]
        parent = parent_ref[b]
        for comp in range(3):
            about[comp, b : b + 1, :] = jnp.full((1, 128), pcent_ref[comp, parent], F32)
    lane = lax.broadcasted_iota(jnp.int32, (NB, 128), 1)

    coords = [rows[comp] for comp in range(3)]
    centers = [jnp.sum(c, axis=1, keepdims=True) * (1.0 / BUCKET) for c in coords]
    sums = monomial_sums([c - o for c, o in zip(coords, centers)], rows[3])
    cells[...] = spread(cell_columns(sums, centers), lane - CELL_LANE)
    parents = [about[comp, :, 0:1] for comp in range(3)]
    sums = monomial_sums([c - o for c, o in zip(coords, parents)], rows[3])
    terms[0] = spread(sums, lane)
    terms[1] = pltpu.roll(terms[0], 35, 1)
    contrib[...] = jnp.zeros(contrib.shape, F32)
    for b in range(NB):
        parent = parent_ref[b]
        row = pl.ds(((parent >> 4) << 3) + (parent & 7), 1)
        contrib[row, :] = contrib[row, :] + terms[(parent >> 3) & 1, b : b + 1, :]

    def fill(step, carry):
        for part in range(4):
            dest = step * 4 + part
            for slot in range(RQ):
                tile = tiles_ref[jnp.maximum(ids_ref[slot, dest], 0)]
                if slot < EARLY:
                    first_ref[dest, slot] = tile
                else:
                    second_ref[dest, slot - EARLY] = tile
            for slot in range(RQC):
                cell = cells[pl.ds(jnp.maximum(cell_ids_ref[slot, dest], 0), 1), :]
                first_ref[dest, EARLY, slot : slot + 1, :] = cell
            own = contrib[pl.ds(pl.multiple_of(dest * 8, 8), 8), :]
            first_ref[dest, EARLY] = first_ref[dest, EARLY] + own
        return carry

    lax.fori_loop(0, chips // 4, fill, 0)


def spread_group(tile_ref, number, spread_ref):
    for r in range(8):
        row = tile_ref[number, r : r + 1, :]
        spread_ref[r] = jnp.transpose(jnp.broadcast_to(row, (128, 128)))


def add_pair(spread_ref, targets, sums, row):
    tx, ty, tz = load_targets(targets, jnp.minimum(row >> 5, 1), row & 31)
    ax, ay, az = [sums[row, comp] for comp in range(3)]
    for h in range(2):
        for g in range(16):
            at = slice(8 * g, 8 * g + 8)
            sx, sy, sz, sm = [spread_ref[2 * comp + h, at, :] for comp in range(4)]
            sx, sy, sz, sm = [jnp.concatenate([v, v], axis=1) for v in (sx, sy, sz, sm)]
            dx = sx - tx
            dy = sy - ty
            dz = sz - tz
            inv = lax.rsqrt(dx * dx + dy * dy + (dz * dz + SOFT_SQ))
            weight = sm * inv * (inv * inv)
            ax = ax + weight * dx
            ay = ay + weight * dy
            az = az + weight * dz
    for comp, value in enumerate((ax, ay, az)):
        sums[row, comp] = value


def list_active(sub, act_ref, order):
    total = 0
    for row in range(2 * NB):
        listed = (sub if row < NB else 1 - sub) * NB + row % NB
        order[total] = row
        total = total + act_ref[listed]
    return total


def listed_row(sub, row):
    return row ^ (sub << 5)


def start_sums(order, total, sums, note, carry):
    def step(n, carry):
        row = order[n]
        for comp in range(3):
            sums[row, comp] = jnp.zeros((8, BUCKET), F32)
        return note(row, carry)

    return lax.fori_loop(0, total, step, carry)


def end_sums(order, total, sums, out_ref):
    def step(n, carry):
        row = order[n]
        add_rows(out_ref, row >> 5, row & 31, [sums[row, comp] for comp in range(3)])
        return carry

    lax.fori_loop(0, total, step, 0)


def load_targets(targets, half, b):
    return [
        jnp.broadcast_to(lanes_of(targets.at[half], comp, b), (8, BUCKET)) for comp in range(3)
    ]


def add_rows(ref, half, b, values):
    at = pl.ds(pl.multiple_of(b * BUCKET, BUCKET), BUCKET)
    for comp in range(3):
        row = jnp.sum(values[comp], axis=0, keepdims=True)
        ref[half, comp : comp + 1, at] = ref[half, comp : comp + 1, at] + row


def local_kernel(
    sub_ref, act_ref, list_ref, near_ref, pos_ref, other_ref, tiles_ref, out_ref, pairs_ref,
    targets, order, sums, one, two, users, counts,
):
    sub = sub_ref[0]
    targets[0] = pos_ref[...]
    targets[1] = other_ref[...]
    out_ref[...] = jnp.zeros(out_ref.shape, F32)
    for comp in range(3):
        sums[2 * NB, comp] = jnp.zeros((8, BUCKET), F32)
    for b in range(NB + 1):
        counts[b] = 0
        users[b * USES] = 2 * NB
    total = list_active(sub, act_ref, order)

    def note(row, carry):
        listed = listed_row(sub, row)
        for k in range(8):
            entry = list_ref[k, listed]
            group = jnp.where((entry >> 5) == sub, entry & 31, NB)
            count = counts[group]
            users[(group << USES_BITS) + count] = row
            counts[group] = count + 1
        early, late = carry
        for k in range(8):
            entry = near_ref[k, listed]
            slot = entry & (RQ - 1)
            mine = jnp.where(((entry >> 2) & 1) == sub, 1, 0)
            soon = jnp.where(slot < EARLY, mine, 0)
            pairs_ref[early] = (entry >> 3) * (EARLY + 1) + slot
            pairs_ref[SPAN + early] = row
            pairs_ref[2 * SPAN + late] = (entry >> 3) * (RQ - EARLY) + slot - EARLY
            pairs_ref[3 * SPAN + late] = row
            early = early + soon
            late = late + (mine - soon)
        return early, late

    early, late = start_sums(order, total, sums, note, (jnp.int32(0), jnp.int32(0)))
    pairs_ref[4 * SPAN] = early
    pairs_ref[4 * SPAN + 1] = late

    def work(group, now, later):
        spread_group(tiles_ref, jnp.minimum(group + 1, NB - 1), later)
        first = group << USES_BITS
        add_pair(now, targets, sums, users[first])

        def more(use, carry):
            add_pair(now, targets, sums, users[first + use])
            return carry

        lax.fori_loop(1, counts[group], more, 0)

    spread_group(tiles_ref, 0, one)

    def step(pair, carry):
        work(2 * pair, one, two)
        work(2 * pair + 1, two, one)
        return carry

    lax.fori_loop(0, NB // 2, step, 0)
    end_sums(order, total, sums, out_ref)


def near_pairs(part, total, pairs_ref, pool_ref, out_ref, scratch):
    targets, order, sums, one, two = scratch
    count = pairs_ref[4 * SPAN + part]

    def name(n):
        return pairs_ref[2 * part * SPAN + jnp.minimum(n, count - 1)]

    def home(n):
        return pairs_ref[(2 * part + 1) * SPAN + n]

    start_sums(order, total, sums, lambda row, carry: carry, 0)

    @pl.when(count > 0)
    def _():
        spread_group(pool_ref, name(0), one)
        spread_group(pool_ref, name(1), two)

        def step(pair, carry):
            add_pair(one, targets, sums, home(2 * pair))
            spread_group(pool_ref, name(2 * pair + 2), one)
            add_pair(two, targets, sums, home(2 * pair + 1))
            spread_group(pool_ref, name(2 * pair + 3), two)
            return carry

        lax.fori_loop(0, count >> 1, step, 0)

        @pl.when((count & 1) == 1)
        def _():
            add_pair(one, targets, sums, home(count - 1))

    end_sums(order, total, sums, out_ref)


def late_kernel(
    sub_ref, act_ref, pairs_ref, pos_ref, other_ref, pool_ref, part_ref, owned_ref, own_ref,
    send_ref, targets, order, sums, one, two, both,
):
    sub = sub_ref[0]
    targets[0] = pos_ref[...]
    targets[1] = other_ref[...]
    both[...] = part_ref[...]
    total = list_active(sub, act_ref, order)
    near_pairs(1, total, pairs_ref, pool_ref, both, (targets, order, sums, one, two))
    own_ref[...] = both[0]
    send_ref[0:3, :] = both[1]
    send_ref[3:4, :] = jnp.zeros((1, send_ref.shape[1]), F32)
    for r in range(8):
        send_ref[3:4, 128 * r : 128 * r + 128] = owned_ref[r : r + 1, :]


def contract(tensor, axis, weighted):
    total = None
    for triple, value in weighted.items():
        term = tensor[plus(triple, AXES[axis])] * value
        total = term if total is None else total + term
    return total


def cell_pull(table, targets):
    def column(number):
        return table[:, CELL_LANE + number : CELL_LANE + number + 1]

    m = {triple: column(number) for number, triple in enumerate(TRIPLES)}
    r = [targets[a] - column(35 + a) for a in range(3)]
    x, y, z = r
    rho_sq = x * x + y * y + (z * z + FAR_SQ)
    inv = lax.rsqrt(rho_sq)
    inv_sq = inv * inv
    u = [inv]
    for _ in range(5):
        u.append(u[-1] * inv_sq)
    xx, yy, zz, xy, xz, yz = x * x, y * y, z * z, x * y, x * z, y * z
    first = {(1, 0, 0): x, (0, 1, 0): y, (0, 0, 1): z}
    second = {
        (2, 0, 0): xx,
        (1, 1, 0): 2.0 * xy,
        (1, 0, 1): 2.0 * xz,
        (0, 2, 0): yy,
        (0, 1, 1): 2.0 * yz,
        (0, 0, 2): zz,
    }
    x3, y3, z3 = 3.0 * x, 3.0 * y, 3.0 * z
    third = {
        (3, 0, 0): xx * x,
        (2, 1, 0): xx * y3,
        (2, 0, 1): xx * z3,
        (1, 2, 0): yy * x3,
        (1, 1, 1): xy * (2.0 * z3),
        (1, 0, 2): zz * x3,
        (0, 3, 0): yy * y,
        (0, 2, 1): yy * z3,
        (0, 1, 2): zz * y3,
        (0, 0, 3): zz * z,
    }
    pairs = [t for t in TRIPLES if sum(t) == 2]
    trace2 = {t: column(42 + number) for number, t in enumerate(pairs)}
    grad = []
    q1, q2, q3, q4 = column(38), column(48), None, None
    for a in range(3):
        m1 = m[AXES[a]]
        a2 = contract(m, a, first)
        b2 = column(39 + a)
        a3 = contract(m, a, second)
        b3 = contract(trace2, a, first)
        a4 = contract(m, a, third)
        grad.append(
            m1 * u[1]
            + (a2 + (a2 - b2)) * u[2]
            + (a3 + 2.0 * (a3 - b3)) * u[3]
            + (4.0 * a4) * u[4]
        )
        q1 = q1 + r[a] * m1
        q2 = q2 + r[a] * (a2 - b2)
        low, high = r[a] * (a3 - b3), r[a] * a4
        q3 = low if q3 is None else q3 + low
        q4 = high if q4 is None else q4 + high
    pull = (
        m[(0, 0, 0)] * u[1] + 3.0 * q1 * u[2] + 5.0 * q2 * u[3] + 7.0 * q3 * u[4] + 9.0 * q4 * u[5]
    )
    return [grad[a] - r[a] * pull for a in range(3)]


def far_cells(sub, total, list_ref, pool_ref, out_ref, targets, order, picked):
    place = lax.broadcasted_iota(jnp.int32, (8, 128), 0)

    def visit(n, carry):
        row = order[n]
        listed = listed_row(sub, row)
        count = 0
        for k in range(16):
            entry = list_ref[k, listed]
            at = pl.ds(count, 1)
            picked[at, :] = pool_ref[(entry >> 4) * (EARLY + 1) + EARLY, pl.ds(entry & (RQC - 1), 1), :]
            count = count + jnp.where(((entry >> 3) & 1) == sub, 1, 0)
        half, b = row >> 5, row & 31
        sides = load_targets(targets, half, b)

        def add_cells(step, sums):
            table = picked[pl.ds(pl.multiple_of(step * 8, 8), 8), :]
            table = jnp.where(place < count - step * 8, table, 0.0)
            return tuple(s + p for s, p in zip(sums, cell_pull(table, sides)))

        zero = jnp.zeros((8, BUCKET), F32)
        sums = lax.fori_loop(0, (count + 7) >> 3, add_cells, (zero, zero, zero))
        add_rows(out_ref, half, b, sums)
        return carry

    lax.fori_loop(0, total, visit, 0)


def early_kernel(
    sub_ref, act_ref, pairs_ref, far_ref, pos_ref, other_ref, pool_ref, part_ref, out_ref,
    owned_ref, targets, order, sums, one, two, picked,
):
    sub = sub_ref[0]
    targets[0] = pos_ref[...]
    targets[1] = other_ref[...]
    out_ref[...] = part_ref[...]

    def gather_owned(step, total):
        for part in range(4):
            total = total + pool_ref[(step * 4 + part) * (EARLY + 1) + EARLY]
        return total

    chips = pool_ref.shape[0] // (EARLY + 1)
    owned_ref[...] = lax.fori_loop(0, chips // 4, gather_owned, jnp.zeros((8, 128), F32))
    total = list_active(sub, act_ref, order)
    far_cells(sub, total, far_ref, pool_ref, out_ref, targets, order, picked)
    near_pairs(0, total, pairs_ref, pool_ref, out_ref, (targets, order, sums, one, two))


def finish_kernel(sub_ref, act_ref, part_ref, came_ref, old_ref, owned_ref, accel_ref, parent_ref):
    sub = sub_ref[0]
    for b in range(NB):
        at = pl.ds(b * BUCKET, BUCKET)
        live = act_ref[sub * NB + b] > 0
        accel_ref[:, at] = jnp.where(live, part_ref[:, at] + came_ref[0:3, at], old_ref[:, at])
    for r in range(8):
        row = owned_ref[r : r + 1, :] + came_ref[3:4, 128 * r : 128 * r + 128]
        parent_ref[r : r + 1, :] = row[:, 0:35]
        parent_ref[8 + r : 9 + r, :] = row[:, 35:70]


def shape(*dims):
    return jax.ShapeDtypeStruct(dims, F32)


def local(
    positions,
    masses,
    old_accel,
    active,
    parent_of,
    parent_centers,
    local_list,
    near_list,
    far_list,
    send_ids,
    cell_send_ids,
):
    chips = lax.axis_size("dom")
    own = NB * BUCKET
    me = lax.axis_index("sub").astype(jnp.int32).reshape(1)
    swap = [(0, 1), (1, 0)]
    near_scratch = [
        pltpu.VMEM((2, 3, own), F32),
        pltpu.SMEM((2 * NB + 8,), jnp.int32),
        pltpu.VMEM((2 * NB + 1, 3, 8, BUCKET), F32),
        pltpu.VMEM((8, 128, 128), F32),
        pltpu.VMEM((8, 128, 128), F32),
    ]
    params = pltpu.CompilerParams(vmem_limit_bytes=32 << 20)

    other = lax.ppermute(positions, "sub", swap)

    tiles, first, second = pl.pallas_call(
        pack_kernel,
        in_specs=[SMEM, SMEM, SMEM, SMEM, VMEM, VMEM],
        out_specs=[VMEM, VMEM, VMEM],
        out_shape=[shape(NB, 8, 128), shape(chips, EARLY + 1, 8, 128), shape(chips, RQ - EARLY, 8, 128)],
        scratch_shapes=[
            pltpu.VMEM((4, NB, BUCKET), F32),
            pltpu.VMEM((3, NB, 128), F32),
            pltpu.VMEM((2, NB, 128), F32),
            pltpu.VMEM((NB, 128), F32),
            pltpu.VMEM((chips * 8, 128), F32),
        ],
        compiler_params=pltpu.CompilerParams(vmem_limit_bytes=60 << 20),
        name="pack",
    )(send_ids[0].T, cell_send_ids[0].T, parent_of, parent_centers, positions, masses.reshape(1, own))

    def exchange(blocks):
        flat = blocks.reshape(chips, -1, 128)
        came = lax.all_to_all(flat, "dom", split_axis=0, concat_axis=0, tiled=True)
        return came.reshape(blocks.shape)

    pool = exchange(first)

    part, pairs = pl.pallas_call(
        local_kernel,
        in_specs=[SMEM, SMEM, SMEM, SMEM, VMEM, VMEM, VMEM],
        out_specs=[VMEM, SMEM],
        out_shape=[shape(2, 3, own), jax.ShapeDtypeStruct((4 * SPAN + 16,), jnp.int32)],
        scratch_shapes=near_scratch
        + [pltpu.SMEM(((NB + 1) * USES,), jnp.int32), pltpu.SMEM((NB + 1,), jnp.int32)],
        compiler_params=params,
        cost_estimate=pl.CostEstimate(flops=2 << 30, transcendentals=1 << 27, bytes_accessed=1 << 20),
        name="near_local",
    )(me, active, local_list.T, near_list.T, positions, other, tiles)

    pool, second, part = lax.optimization_barrier((pool, second, part))
    late_pool = exchange(second)

    part, owned = pl.pallas_call(
        early_kernel,
        in_specs=[SMEM, SMEM, SMEM, SMEM, VMEM, VMEM, VMEM, VMEM],
        out_specs=[VMEM, VMEM],
        out_shape=[shape(2, 3, own), shape(8, 128)],
        scratch_shapes=near_scratch + [pltpu.VMEM((24, 128), F32)],
        compiler_params=params,
        cost_estimate=pl.CostEstimate(flops=2 << 30, transcendentals=1 << 27, bytes_accessed=1 << 20),
        name="early",
    )(me, active, pairs, far_list.T, positions, other, pool.reshape(-1, 8, 128), part)
    part, send = pl.pallas_call(
        late_kernel,
        in_specs=[SMEM, SMEM, SMEM, VMEM, VMEM, VMEM, VMEM, VMEM],
        out_specs=[VMEM, VMEM],
        out_shape=[shape(3, own), shape(4, own)],
        scratch_shapes=near_scratch + [pltpu.VMEM((2, 3, own), F32)],
        compiler_params=params,
        cost_estimate=pl.CostEstimate(flops=1 << 30, transcendentals=1 << 26, bytes_accessed=1 << 20),
        name="late",
    )(me, active, pairs, positions, other, late_pool.reshape(-1, 8, 128), part, owned)

    came = lax.ppermute(send, "sub", swap)
    accel, parents = pl.pallas_call(
        finish_kernel,
        in_specs=[SMEM, SMEM, VMEM, VMEM, VMEM, VMEM],
        out_specs=[VMEM, VMEM],
        out_shape=[shape(3, own), shape(16, 35)],
        compiler_params=params,
        name="finish",
    )(me, active, part, came, old_accel, owned)
    return accel, parents.T


def solution(mesh):
    both = ("dom", "sub")
    in_specs = (
        P(None, both),
        P(both),
        P(None, both),
        P("dom"),
        P(both),
        P(),
        P("dom", None),
        P("dom", None),
        P("dom", None),
        P(both, None, None),
        P(both, None, None),
    )
    out_specs = (P(None, both), P(None, "dom"))
    return jax.shard_map(local, mesh=mesh, in_specs=in_specs, out_specs=out_specs, check_vma=False)
```

profile of v0, /device:TPU:1, one launch (start us, length us, event | category | flops | bytes accessed | tf_op | source)
XLA Modules:
  0.0 108.3 jit_solution(18393498761500700221)
XLA Ops:
  0.6 6.4 %pack.1 = (f32[32,8,128]{2,1,0:T(8,128)}, f32[128,3,8,128]{3,2,1,0:T(8,128)}, f32[128,2,8,128]{3,2,1,0:T(8,128)}) custom-call(s32[4,128]{1,0:T(4,128)} %bitcast.26, s32[8,128]{1,0:T(8,128)} %bitcast.25, s32[32]{0:T(128)} %parent_ref.1, f32[3,2048]{1,0:T(4,128)} %pcent_ref.1, f32[3,8192]{1,0:T(4,128)} %pos_ref.7, f32[1,8192]{1,0:T(1,128)} %bitcast.24), custom_call_target="tpu_custom_call" | custom-call | tf_op jit(solution)/shard_map/pack/pallas_call | solution.py:495
  7.0 0.0 copy-start.1
  7.1 0.0 copy-start.2
  7.1 0.0 copy-start.3
  7.1 0.0 copy-start.5
  7.1 0.0 copy-start.6
  7.1 16.5 %all-to-all-start = ((f32[128,24,128]{2,1,0:T(8,128)}), f32[128,24,128]{2,1,0:T(8,128)S(1)}, u32[]{:S(2)}, u32[]{:S(2)}) async-start(f32[128,24,128]{2,1,0:T(8,128)} %bitcast.22), calls=%async_computation | async-start | bytes 3145728 | tf_op jit(solution)/shard_map/all_to_all | solution.py:513
  23.6 0.0 copy-done.1
  23.6 1.0 collective-permute-start
  24.6 1.0 collective-permute-done.other_ref
  25.6 0.0 copy-done.2
  25.6 0.0 copy-done.3
  25.6 0.0 copy-done.5
  25.6 0.0 copy-done.6
  25.6 17.6 %near_local.1 = (f32[2,3,8192]{2,1,0:T(4,128)S(1)}, s32[2128]{0:T(1024)S(1)}) custom-call(s32[1]{0:T(128)} %bitcast.sub_ref, s32[64]{0:T(128)S(1)} %copy-done.2, s32[8,64]{1,0:T(8,128)S(1)} %bitcast.20, s32[8,64]{1,0:T(8,128)S(1)} %bitcast.21, f32[3,8192]{1,0:T(4,128)S(1)} %copy-done.1, f32[3,8192]{1,0:T(4,128)S(1)} %collective-permute-done.other_ref, ...), custom_call_target="tpu_custom_call" | custom-call | flops 2147483648 | bytes 1048576 | tf_op jit(solution)/shard_map/near_local/pallas_call | solution.py:518
  43.3 0.0 copy-start.4
  43.3 19.0 %all-to-all-done = f32[128,24,128]{2,1,0:T(8,128)S(1)} async-done(((f32[128,24,128]{2,1,0:T(8,128)}), f32[128,24,128]{2,1,0:T(8,128)S(1)}, u32[]{:S(2)}, u32[]{:S(2)}) %all-to-all-start) | async-done | bytes 1572896 | tf_op jit(solution)/shard_map/all_to_all | solution.py:513
  62.3 8.9 %all-to-all-start.1 = ((f32[128,16,128]{2,1,0:T(8,128)}), f32[128,16,128]{2,1,0:T(8,128)S(1)}, u32[]{:S(2)}, u32[]{:S(2)}) async-start(f32[128,16,128]{2,1,0:T(8,128)} %bitcast.23), calls=%async_computation.1 | async-start | bytes 2097152 | tf_op jit(solution)/shard_map/all_to_all | solution.py:513
  71.3 0.0 copy-done.4
  71.3 18.0 %early.1 = (f32[2,3,8192]{2,1,0:T(4,128)S(1)}, f32[8,128]{1,0:T(8,128)S(1)}) custom-call(s32[1]{0:T(128)} %bitcast.sub_ref, s32[64]{0:T(128)S(1)} %copy-done.2, s32[2128]{0:T(1024)S(1)} %get-tuple-element.17.pairs_ref, s32[16,64]{1,0:T(8,128)S(1)} %bitcast.19, f32[3,8192]{1,0:T(4,128)S(1)} %copy-done.1, f32[3,8192]{1,0:T(4,128)S(1)} %collective-permute-done.other_ref, ...), custom_call_target="tpu_custom_call" | custom-call | flops 2147483648 | bytes 1048576 | tf_op jit(solution)/shard_map/early/pallas_call | solution.py:533
  89.2 8.4 %all-to-all-done.1 = f32[128,16,128]{2,1,0:T(8,128)S(1)} async-done(((f32[128,16,128]{2,1,0:T(8,128)}), f32[128,16,128]{2,1,0:T(8,128)S(1)}, u32[]{:S(2)}, u32[]{:S(2)}) %all-to-all-start.1) | async-done | bytes 1048608 | tf_op jit(solution)/shard_map/all_to_all | solution.py:513
  97.6 0.0 copy-start
  97.7 3.3 %late.1 = (f32[3,8192]{1,0:T(4,128)S(1)}, f32[4,8192]{1,0:T(4,128)S(1)}) custom-call(s32[1]{0:T(128)} %bitcast.sub_ref, s32[64]{0:T(128)S(1)} %copy-done.2, s32[2128]{0:T(1024)S(1)} %get-tuple-element.17.pairs_ref, f32[3,8192]{1,0:T(4,128)S(1)} %copy-done.1, f32[3,8192]{1,0:T(4,128)S(1)} %collective-permute-done.other_ref, f32[256,8,128]{2,1,0:T(8,128)S(1)} %bitcast.18, ...), custom_call_target="tpu_custom_call" | custom-call | flops 1073741824 | bytes 1048576 | tf_op jit(solution)/shard_map/late/pallas_call | solution.py:543
  100.9 5.1 %collective-permute-start.1 = (f32[4,8192]{1,0:T(4,128)S(1)}, f32[4,8192]{1,0:T(4,128)S(1)}, u32[]{:S(2)}, u32[]{:S(2)}) collective-permute-start(f32[4,8192]{1,0:T(4,128)S(1)} %get-tuple-element.27), channel_id=1, source_target_pairs={{0,1},{1,0},{2,3},{3,2},{4,5},{5,4},{6,7},{7,6},{8,9},{9,8},{10,11... | collective-permute-start | bytes 393224 | tf_op jit(solution)/shard_map/ppermute | solution.py:554
  106.0 1.0 collective-permute-done.1.came_ref
  107.0 0.0 copy-done
  107.0 1.2 %finish.1 = (f32[3,8192]{1,0:T(4,128)}, f32[16,35]{1,0:T(8,128)}) custom-call(s32[1]{0:T(128)} %bitcast.sub_ref, s32[64]{0:T(128)S(1)} %copy-done.2, f32[3,8192]{1,0:T(4,128)S(1)} %get-tuple-element.26.part_ref, f32[4,8192]{1,0:T(4,128)S(1)} %collective-permute-done.1.came_ref, f32[3,8192]{1,0:T(4,128)S(1)} %copy-done, f32[8,128]{1,0:T(8,128)S(1)} %get-tuple-element.25.owned_ref), custom_call_target="tpu_custom_call" | custom-call | tf_op jit(solution)/shard_map/finish/pallas_call | solution.py:555
Async XLA Ops:
  7.0 16.5 %copy-start.1 = (f32[3,8192]{1,0:T(4,128)S(1)}, f32[3,8192]{1,0:T(4,128)}, u32[]{:S(2)}) copy-start(f32[3,8192]{1,0:T(4,128)} %pos_ref.7) | copy-start | bytes 294916
  7.1 18.6 %copy-start.2 = (s32[64]{0:T(128)S(1)}, s32[64]{0:T(128)}, u32[]{:S(2)}) copy-start(s32[64]{0:T(128)} %act_ref.7) | copy-start | bytes 772
  7.1 18.6 %copy-start.3 = (f32[32,8,128]{2,1,0:T(8,128)S(1)}, f32[32,8,128]{2,1,0:T(8,128)}, u32[]{:S(2)}) copy-start(f32[32,8,128]{2,1,0:T(8,128)} %get-tuple-element.16.tiles_ref) | copy-start | bytes 393220
  7.1 18.6 %copy-start.5 = (s32[64,8]{0,1:T(8,128)S(1)}, s32[64,8]{0,1:T(8,128)}, u32[]{:S(2)}) copy-start(s32[64,8]{0,1:T(8,128)} %param.17) | copy-start | bytes 6148
  7.1 18.5 %copy-start.6 = (s32[64,8]{0,1:T(8,128)S(1)}, s32[64,8]{0,1:T(8,128)}, u32[]{:S(2)}) copy-start(s32[64,8]{0,1:T(8,128)} %param.18) | copy-start | bytes 6148
  7.1 55.2 %all-to-all-start = ((f32[128,24,128]{2,1,0:T(8,128)}), f32[128,24,128]{2,1,0:T(8,128)S(1)}, u32[]{:S(2)}, u32[]{:S(2)}) async-start(f32[128,24,128]{2,1,0:T(8,128)} %bitcast.22), calls=%async_computation | async-start | bytes 3145728 | tf_op jit(solution)/shard_map/all_to_all | solution.py:513
  23.6 2.0 %collective-permute-start = (f32[3,8192]{1,0:T(4,128)S(1)}, f32[3,8192]{1,0:T(4,128)S(1)}, u32[]{:S(2)}, u32[]{:S(2)}) collective-permute-start(f32[3,8192]{1,0:T(4,128)S(1)} %copy-done.1), channel_id=1, source_target_pairs={{0,1},{1,0},{2,3},{3,2},{4,5},{5,4},{6,7},{7,6},{8,9},{9,8},{10,11... | collective-permute-start | bytes 294920 | tf_op jit(solution)/shard_map/ppermute | solution.py:493
  43.3 28.0 %copy-start.4 = (s32[64,16]{0,1:T(8,128)S(1)}, s32[64,16]{0,1:T(8,128)}, u32[]{:S(2)}) copy-start(s32[64,16]{0,1:T(8,128)} %param.19) | copy-start | bytes 12292
  62.3 35.3 %all-to-all-start.1 = ((f32[128,16,128]{2,1,0:T(8,128)}), f32[128,16,128]{2,1,0:T(8,128)S(1)}, u32[]{:S(2)}, u32[]{:S(2)}) async-start(f32[128,16,128]{2,1,0:T(8,128)} %bitcast.23), calls=%async_computation.1 | async-start | bytes 2097152 | tf_op jit(solution)/shard_map/all_to_all | solution.py:513
  97.6 9.4 %copy-start = (f32[3,8192]{1,0:T(4,128)S(1)}, f32[3,8192]{1,0:T(4,128)}, u32[]{:S(2)}) copy-start(f32[3,8192]{1,0:T(4,128)} %old_ref.1) | copy-start | bytes 294916
  100.9 6.1 %collective-permute-start.1 = (f32[4,8192]{1,0:T(4,128)S(1)}, f32[4,8192]{1,0:T(4,128)S(1)}, u32[]{:S(2)}, u32[]{:S(2)}) collective-permute-start(f32[4,8192]{1,0:T(4,128)S(1)} %get-tuple-element.27), channel_id=1, source_target_pairs={{0,1},{1,0},{2,3},{3,2},{4,5},{5,4},{6,7},{7,6},{8,9},{9,8},{10,11... | collective-permute-start | bytes 393224 | tf_op jit(solution)/shard_map/ppermute | solution.py:554
where the time goes:
time: 109 us; the launch traced here: 108 us
  Pallas kernels  46.5 us (43%)
  starting transfers between devices  31.5 us (29%)
  waiting for transfers between devices  29.4 us (27%)
    all_to_all x2, waiting for transfers between devices, exchange(): came = lax.all_to_all(flat, 'dom', split_axis=0, concat_axis=0, tiled=True)  27.5 us
    all_to_all x2, starting transfers between devices, exchange(): came = lax.all_to_all(flat, 'dom', split_axis=0, concat_axis=0, tiled=True)  25.4 us
    pallas_call x1, Pallas kernels, local(): pl.pallas_call(early_kernel, in_specs=[SMEM, SMEM, SMEM, SMEM, VMEM, VMEM...  18 us
    pallas_call x1, Pallas kernels, local(): pl.pallas_call(local_kernel, in_specs=[SMEM, SMEM, SMEM, SMEM, VMEM, VMEM...  17.6 us
    pallas_call x1, Pallas kernels, local(): pl.pallas_call(pack_kernel, in_specs=[SMEM, SMEM, SMEM, SMEM, VMEM, VMEM]...  6.42 us
    ppermute x1, starting transfers between devices, local(): came = lax.ppermute(send, 'sub', swap)  5.09 us
    pallas_call x1, Pallas kernels, local(): pl.pallas_call(late_kernel, in_specs=[SMEM, SMEM, SMEM, VMEM, VMEM, VMEM,...  3.29 us
  transfers between devices with their start and end apart: 4, of which 4 were waited for; matrix products, arithmetic and copies ran while one was open for 0% of the time, Pallas kernels for 33%

commit v1 on v0

--- a/solution.py
+++ b/solution.py
@@ -45,6 +45,18 @@
     return ref[comp : comp + 1, pl.ds(pl.multiple_of(b * BUCKET, BUCKET), BUCKET)]
 
 
+def pack_late_kernel(ids_ref, tiles_ref, second_ref):
+    def fill(step, carry):
+        for part in range(4):
+            dest = step * 4 + part
+            for slot in range(EARLY, RQ):
+                group = jnp.maximum(ids_ref[slot, dest], 0)
+                second_ref[dest, slot - EARLY] = tiles_ref[group]
+        return carry
+
+    lax.fori_loop(0, second_ref.shape[0] // 4, fill, 0)
+
+
 def monomial_sums(offsets, mass):
     x, y, z = offsets
     known = {(0, 0, 0): mass}
@@ -90,7 +102,6 @@
     mass_ref,
     tiles_ref,
     first_ref,
-    second_ref,
     rows,
     about,
     terms,
@@ -127,12 +138,8 @@
     def fill(step, carry):
         for part in range(4):
             dest = step * 4 + part
-            for slot in range(RQ):
-                tile = tiles_ref[jnp.maximum(ids_ref[slot, dest], 0)]
-                if slot < EARLY:
-                    first_ref[dest, slot] = tile
-                else:
-                    second_ref[dest, slot - EARLY] = tile
+            for slot in range(EARLY):
+                first_ref[dest, slot] = tiles_ref[jnp.maximum(ids_ref[slot, dest], 0)]
             for slot in range(RQC):
                 cell = cells[pl.ds(jnp.maximum(cell_ids_ref[slot, dest], 0), 1), :]
                 first_ref[dest, EARLY, slot : slot + 1, :] = cell
@@ -492,11 +499,11 @@
 
     other = lax.ppermute(positions, "sub", swap)
 
-    tiles, first, second = pl.pallas_call(
+    tiles, first = pl.pallas_call(
         pack_kernel,
         in_specs=[SMEM, SMEM, SMEM, SMEM, VMEM, VMEM],
-        out_specs=[VMEM, VMEM, VMEM],
-        out_shape=[shape(NB, 8, 128), shape(chips, EARLY + 1, 8, 128), shape(chips, RQ - EARLY, 8, 128)],
+        out_specs=[VMEM, VMEM],
+        out_shape=[shape(NB, 8, 128), shape(chips, EARLY + 1, 8, 128)],
         scratch_shapes=[
             pltpu.VMEM((4, NB, BUCKET), F32),
             pltpu.VMEM((3, NB, 128), F32),
@@ -527,6 +534,15 @@
         name="near_local",
     )(me, active, local_list.T, near_list.T, positions, other, tiles)
 
+    second = pl.pallas_call(
+        pack_late_kernel,
+        in_specs=[SMEM, VMEM],
+        out_specs=VMEM,
+        out_shape=shape(chips, RQ - EARLY, 8, 128),
+        compiler_params=params,
+        cost_estimate=pl.CostEstimate(flops=1 << 20, transcendentals=0, bytes_accessed=2 << 20),
+        name="pack_late",
+    )(send_ids[0].T, tiles)
     pool, second, part = lax.optimization_barrier((pool, second, part))
     late_pool = exchange(second)
 

time: 109 us -> 109 us (level); the launches traced: 108 us -> 107 us
  Pallas kernels: 46.5 us -> 43.9 us
  waiting for transfers between devices: 29.4 us -> 30.9 us
    all_to_all x2, waiting for transfers between devices: 27.5 us -> 29.9 us  [exchange(): came = lax.all_to_all(flat, 'dom', split_axis=0, concat_axis=0, tiled=True)]
    pallas_call x0 -> x1, Pallas kernels: none -> 2.27 us  [local(): pl.pallas_call(pack_late_kernel, in_specs=[SMEM, VMEM], out_specs=VMEM, o...]
    pallas_call x1, Pallas kernels: 18 us -> 16 us  [local(): pl.pallas_call(early_kernel, in_specs=[SMEM, SMEM, SMEM, SMEM, VMEM, VMEM...]
    pallas_call x1, Pallas kernels: 17.6 us -> 15.8 us  [local(): pl.pallas_call(local_kernel, in_specs=[SMEM, SMEM, SMEM, SMEM, VMEM, VMEM...]
  transfers between devices with their start and end apart: 4 -> 4, of which waited for: 4 -> 3; matrix products, arithmetic and copies ran while one was open for 0% -> 0% of each run, Pallas kernels for 33% -> 32%
where the time goes in v1:
time: 109 us; the launch traced here: 107 us
  Pallas kernels  43.9 us (40%)
  starting transfers between devices  31.5 us (29%)
  waiting for transfers between devices  30.9 us (28%)
    all_to_all x2, waiting for transfers between devices, exchange(): came = lax.all_to_all(flat, 'dom', split_axis=0, concat_axis=0, tiled=True)  29.9 us
    all_to_all x2, starting transfers between devices, exchange(): came = lax.all_to_all(flat, 'dom', split_axis=0, concat_axis=0, tiled=True)  25.4 us
    pallas_call x1, Pallas kernels, local(): pl.pallas_call(early_kernel, in_specs=[SMEM, SMEM, SMEM, SMEM, VMEM, VMEM...  16 us
    pallas_call x1, Pallas kernels, local(): pl.pallas_call(local_kernel, in_specs=[SMEM, SMEM, SMEM, SMEM, VMEM, VMEM...  15.8 us
    pallas_call x1, Pallas kernels, local(): pl.pallas_call(pack_kernel, in_specs=[SMEM, SMEM, SMEM, SMEM, VMEM, VMEM]...  5.7 us
    ppermute x1, starting transfers between devices, local(): came = lax.ppermute(send, 'sub', swap)  5.08 us
    pallas_call x1, Pallas kernels, local(): pl.pallas_call(late_kernel, in_specs=[SMEM, SMEM, SMEM, VMEM, VMEM, VMEM,...  2.87 us
    pallas_call x1, Pallas kernels, local(): pl.pallas_call(pack_late_kernel, in_specs=[SMEM, VMEM], out_specs=VMEM, o...  2.27 us
  transfers between devices with their start and end apart: 4, of which 3 were waited for; matrix products, arithmetic and copies ran while one was open for 0% of the time, Pallas kernels for 32%

profile of v1, /device:TPU:1, one launch (start us, length us, event | category | flops | bytes accessed | tf_op | source)
XLA Modules:
  0.0 107.1 jit_solution(7972086573313860033)
XLA Ops:
  0.6 5.7 %pack.1 = (f32[32,8,128]{2,1,0:T(8,128)}, f32[128,3,8,128]{3,2,1,0:T(8,128)}) custom-call(s32[4,128]{1,0:T(4,128)} %bitcast.19, s32[8,128]{1,0:T(8,128)} %bitcast.26, s32[32]{0:T(128)} %parent_ref.1, f32[3,2048]{1,0:T(4,128)} %pcent_ref.1, f32[3,8192]{1,0:T(4,128)} %pos_ref.7, f32[1,8192]{1,0:T(1,128)} %bitcast.25), custom_call_target="tpu_custom_call" | custom-call | tf_op jit(solution)/shard_map/pack/pallas_call | solution.py:502
  6.3 0.0 copy-start.2
  6.3 0.0 copy-start.1
  6.3 0.0 copy-start.3
  6.3 0.0 copy-start.4
  6.4 0.0 copy-start.6
  6.4 0.0 copy-start.7
  6.4 16.5 %all-to-all-start = ((f32[128,24,128]{2,1,0:T(8,128)}), f32[128,24,128]{2,1,0:T(8,128)S(1)}, u32[]{:S(2)}, u32[]{:S(2)}) async-start(f32[128,24,128]{2,1,0:T(8,128)} %bitcast.24), calls=%async_computation | async-start | bytes 3145728 | tf_op jit(solution)/shard_map/all_to_all | solution.py:520
  22.9 0.0 copy-done.2
  22.9 1.0 collective-permute-start
  23.9 0.0 copy-done.1
  23.9 0.0 copy-done.3
  23.9 2.3 %pack_late.1 = f32[128,2,8,128]{3,2,1,0:T(8,128)} custom-call(s32[4,128]{1,0:T(4,128)S(1)} %bitcast.20, f32[32,8,128]{2,1,0:T(8,128)S(1)} %copy-done.1), custom_call_target="tpu_custom_call" | custom-call | flops 1048576 | bytes 2097152 | tf_op jit(solution)/shard_map/pack_late/pallas_call | solution.py:537
  26.2 0.0 collective-permute-done.other_ref
  26.2 0.0 copy-done.4
  26.2 0.0 copy-done.6
  26.2 0.0 copy-done.7
  26.2 15.8 %near_local.1 = (f32[2,3,8192]{2,1,0:T(4,128)S(1)}, s32[2128]{0:T(1024)S(1)}) custom-call(s32[1]{0:T(128)} %bitcast.sub_ref, s32[64]{0:T(128)S(1)} %copy-done.4, s32[8,64]{1,0:T(8,128)S(1)} %bitcast.22, s32[8,64]{1,0:T(8,128)S(1)} %bitcast.23, f32[3,8192]{1,0:T(4,128)S(1)} %copy-done.2, f32[3,8192]{1,0:T(4,128)S(1)} %collective-permute-done.other_ref, ...), custom_call_target="tpu_custom_call" | custom-call | flops 2147483648 | bytes 1048576 | tf_op jit(solution)/shard_map/near_local/pallas_call | solution.py:525
  42.1 0.0 copy-start.5
  42.1 19.6 %all-to-all-done = f32[128,24,128]{2,1,0:T(8,128)S(1)} async-done(((f32[128,24,128]{2,1,0:T(8,128)}), f32[128,24,128]{2,1,0:T(8,128)S(1)}, u32[]{:S(2)}, u32[]{:S(2)}) %all-to-all-start) | async-done | bytes 1572896 | tf_op jit(solution)/shard_map/all_to_all | solution.py:520
  61.6 8.9 %all-to-all-start.1 = ((f32[128,16,128]{2,1,0:T(8,128)}), f32[128,16,128]{2,1,0:T(8,128)S(1)}, u32[]{:S(2)}, u32[]{:S(2)}) async-start(f32[128,16,128]{2,1,0:T(8,128)} %bitcast.11), calls=%async_computation.1 | async-start | bytes 2097152 | tf_op jit(solution)/shard_map/all_to_all | solution.py:520
  70.6 0.0 copy-done.5
  70.6 16.0 %early.1 = (f32[2,3,8192]{2,1,0:T(4,128)S(1)}, f32[8,128]{1,0:T(8,128)S(1)}) custom-call(s32[1]{0:T(128)} %bitcast.sub_ref, s32[64]{0:T(128)S(1)} %copy-done.4, s32[2128]{0:T(1024)S(1)} %get-tuple-element.16.pairs_ref, s32[16,64]{1,0:T(8,128)S(1)} %bitcast.21, f32[3,8192]{1,0:T(4,128)S(1)} %copy-done.2, f32[3,8192]{1,0:T(4,128)S(1)} %collective-permute-done.other_ref, ...), custom_call_target="tpu_custom_call" | custom-call | flops 2147483648 | bytes 1048576 | tf_op jit(solution)/shard_map/early/pallas_call | solution.py:549
  86.6 10.4 %all-to-all-done.1 = f32[128,16,128]{2,1,0:T(8,128)S(1)} async-done(((f32[128,16,128]{2,1,0:T(8,128)}), f32[128,16,128]{2,1,0:T(8,128)S(1)}, u32[]{:S(2)}, u32[]{:S(2)}) %all-to-all-start.1) | async-done | bytes 1048608 | tf_op jit(solution)/shard_map/all_to_all | solution.py:520
  96.9 0.0 copy-start
  96.9 2.9 %late.1 = (f32[3,8192]{1,0:T(4,128)S(1)}, f32[4,8192]{1,0:T(4,128)S(1)}) custom-call(s32[1]{0:T(128)} %bitcast.sub_ref, s32[64]{0:T(128)S(1)} %copy-done.4, s32[2128]{0:T(1024)S(1)} %get-tuple-element.16.pairs_ref, f32[3,8192]{1,0:T(4,128)S(1)} %copy-done.2, f32[3,8192]{1,0:T(4,128)S(1)} %collective-permute-done.other_ref, f32[256,8,128]{2,1,0:T(8,128)S(1)} %bitcast.18, ...), custom_call_target="tpu_custom_call" | custom-call | flops 1073741824 | bytes 1048576 | tf_op jit(solution)/shard_map/late/pallas_call | solution.py:559
  99.8 5.1 %collective-permute-start.1 = (f32[4,8192]{1,0:T(4,128)S(1)}, f32[4,8192]{1,0:T(4,128)S(1)}, u32[]{:S(2)}, u32[]{:S(2)}) collective-permute-start(f32[4,8192]{1,0:T(4,128)S(1)} %get-tuple-element.25), channel_id=1, source_target_pairs={{0,1},{1,0},{2,3},{3,2},{4,5},{5,4},{6,7},{7,6},{8,9},{9,8},{10,11... | collective-permute-start | bytes 393224 | tf_op jit(solution)/shard_map/ppermute | solution.py:570
  104.9 1.0 collective-permute-done.1.came_ref
  105.9 0.0 copy-done
  105.9 1.2 %finish.1 = (f32[3,8192]{1,0:T(4,128)}, f32[16,35]{1,0:T(8,128)}) custom-call(s32[1]{0:T(128)} %bitcast.sub_ref, s32[64]{0:T(128)S(1)} %copy-done.4, f32[3,8192]{1,0:T(4,128)S(1)} %get-tuple-element.24.part_ref, f32[4,8192]{1,0:T(4,128)S(1)} %collective-permute-done.1.came_ref, f32[3,8192]{1,0:T(4,128)S(1)} %copy-done, f32[8,128]{1,0:T(8,128)S(1)} %get-tuple-element.23.owned_ref), custom_call_target="tpu_custom_call" | custom-call | tf_op jit(solution)/shard_map/finish/pallas_call | solution.py:571
Async XLA Ops:
  6.3 16.5 %copy-start.2 = (f32[3,8192]{1,0:T(4,128)S(1)}, f32[3,8192]{1,0:T(4,128)}, u32[]{:S(2)}) copy-start(f32[3,8192]{1,0:T(4,128)} %pos_ref.7) | copy-start | bytes 294916
  6.3 17.6 %copy-start.1 = (f32[32,8,128]{2,1,0:T(8,128)S(1)}, f32[32,8,128]{2,1,0:T(8,128)}, u32[]{:S(2)}) copy-start(f32[32,8,128]{2,1,0:T(8,128)} %get-tuple-element.15.tiles_ref) | copy-start | bytes 393220
  6.3 17.6 %copy-start.3 = (s32[1,128,4]{1,2,0:T(4,128)S(1)}, s32[1,128,4]{1,2,0:T(4,128)}, u32[]{:S(2)}) copy-start(s32[1,128,4]{1,2,0:T(4,128)} %param.20) | copy-start | bytes 6148
  6.3 19.9 %copy-start.4 = (s32[64]{0:T(128)S(1)}, s32[64]{0:T(128)}, u32[]{:S(2)}) copy-start(s32[64]{0:T(128)} %act_ref.7) | copy-start | bytes 772
  6.4 19.8 %copy-start.6 = (s32[64,8]{0,1:T(8,128)S(1)}, s32[64,8]{0,1:T(8,128)}, u32[]{:S(2)}) copy-start(s32[64,8]{0,1:T(8,128)} %param.17) | copy-start | bytes 6148
  6.4 19.8 %copy-start.7 = (s32[64,8]{0,1:T(8,128)S(1)}, s32[64,8]{0,1:T(8,128)}, u32[]{:S(2)}) copy-start(s32[64,8]{0,1:T(8,128)} %param.18) | copy-start | bytes 6148
  6.4 55.2 %all-to-all-start = ((f32[128,24,128]{2,1,0:T(8,128)}), f32[128,24,128]{2,1,0:T(8,128)S(1)}, u32[]{:S(2)}, u32[]{:S(2)}) async-start(f32[128,24,128]{2,1,0:T(8,128)} %bitcast.24), calls=%async_computation | async-start | bytes 3145728 | tf_op jit(solution)/shard_map/all_to_all | solution.py:520
  22.9 3.3 %collective-permute-start = (f32[3,8192]{1,0:T(4,128)S(1)}, f32[3,8192]{1,0:T(4,128)S(1)}, u32[]{:S(2)}, u32[]{:S(2)}) collective-permute-start(f32[3,8192]{1,0:T(4,128)S(1)} %copy-done.2), channel_id=1, source_target_pairs={{0,1},{1,0},{2,3},{3,2},{4,5},{5,4},{6,7},{7,6},{8,9},{9,8},{10,11... | collective-permute-start | bytes 294920 | tf_op jit(solution)/shard_map/ppermute | solution.py:500
  42.1 28.5 %copy-start.5 = (s32[64,16]{0,1:T(8,128)S(1)}, s32[64,16]{0,1:T(8,128)}, u32[]{:S(2)}) copy-start(s32[64,16]{0,1:T(8,128)} %param.19) | copy-start | bytes 12292
  61.6 35.3 %all-to-all-start.1 = ((f32[128,16,128]{2,1,0:T(8,128)}), f32[128,16,128]{2,1,0:T(8,128)S(1)}, u32[]{:S(2)}, u32[]{:S(2)}) async-start(f32[128,16,128]{2,1,0:T(8,128)} %bitcast.11), calls=%async_computation.1 | async-start | bytes 2097152 | tf_op jit(solution)/shard_map/all_to_all | solution.py:520
  96.9 9.0 %copy-start = (f32[3,8192]{1,0:T(4,128)S(1)}, f32[3,8192]{1,0:T(4,128)}, u32[]{:S(2)}) copy-start(f32[3,8192]{1,0:T(4,128)} %old_ref.1) | copy-start | bytes 294916
  99.8 6.1 %collective-permute-start.1 = (f32[4,8192]{1,0:T(4,128)S(1)}, f32[4,8192]{1,0:T(4,128)S(1)}, u32[]{:S(2)}, u32[]{:S(2)}) collective-permute-start(f32[4,8192]{1,0:T(4,128)S(1)} %get-tuple-element.25), channel_id=1, source_target_pairs={{0,1},{1,0},{2,3},{3,2},{4,5},{5,4},{6,7},{7,6},{8,9},{9,8},{10,11... | collective-permute-start | bytes 393224 | tf_op jit(solution)/shard_map/ppermute | solution.py:570
